TPU v7x, 32 devices: a whole 2x2x4 slice. The times are simulated.
32 devices in a mesh: dev: 2 (over x), sa: 16 (over z, y, core).
Axes of the slice: x: 2, y: 2, z: 4, core: 2. Of those that a mesh axis runs over, the one named last changes fastest.
Arguments:
- patches: bfloat16 [8, 1024, 1152], P('dev', 'sa'), may hold values from -6 to 6
- patch_mask: int32 [8, 1024], P('dev', 'sa'), may hold values from 0 to 1, as said below
- cotangent: bfloat16 [8, 1024, 1152], P('dev', 'sa'), may hold values from -6 to 6
- w_qkv: bfloat16 [1152, 3456], P('sa', 'dev'), may hold values from -0.1875 to 0.1875
- w_out: bfloat16 [1152, 1152], P('sa', 'dev'), may hold values from -0.75 to 0.75
- w_up: bfloat16 [1152, 4304], P('sa', 'dev'), may hold values from -0.1875 to 0.1875
- w_down: bfloat16 [1152, 4304], P('sa', 'dev'), may hold values from -0.125 to 0.125
- gain_one: bfloat16 [1, 1152], P(None, 'dev'), may hold values from 0.25 to 1.75
- shift_one: bfloat16 [1, 1152], P(None, 'dev'), may hold values from -4 to 4
- gain_two: bfloat16 [1, 1152], P(None, 'dev'), may hold values from 0.25 to 1.75
- shift_two: bfloat16 [1, 1152], P(None, 'dev'), may hold values from -4 to 4
- bias_query: bfloat16 [1, 1152], P(None, 'dev'), may hold values from -4 to 4
- bias_value: bfloat16 [1, 1152], P(None, 'dev'), may hold values from -4 to 4
- bias_out: bfloat16 [1, 1152], P(None, 'dev'), may hold values from -4 to 4
- bias_up: bfloat16 [1, 4304], P(None, 'dev'), may hold values from -4 to 4
- bias_down: bfloat16 [1, 1152], P(None, 'dev'), may hold values from -4 to 4
Outputs:
- result: bfloat16 [8, 1024, 1152], P('dev', 'sa')
- grad_patches: bfloat16 [8, 1024, 1152], P('dev', 'sa')
- grad_w_qkv: float32 [1152, 3456], P('sa', 'dev')
- grad_w_out: float32 [1152, 1152], P('sa', 'dev')
- grad_w_up: float32 [1152, 4304], P('sa', 'dev')
- grad_w_down: float32 [1152, 4304], P('sa', 'dev')
- grad_gain_one: float32 [1, 1152], P(None, 'dev')
- grad_shift_one: float32 [1, 1152], P(None, 'dev')
- grad_gain_two: float32 [1, 1152], P(None, 'dev')
- grad_shift_two: float32 [1, 1152], P(None, 'dev')
- grad_bias_query: float32 [1, 1152], P(None, 'dev')
- grad_bias_value: float32 [1, 1152], P(None, 'dev')
- grad_bias_out: float32 [1, 1152], P(None, 'dev')
- grad_bias_up: float32 [1, 4304], P(None, 'dev')
- grad_bias_down: float32 [1, 1152], P(None, 'dev')
Inputs may be any that keep to these rules, and one draw needn't show every extreme that they name: `patch_mask`: each image's ones are its first patches, 256 of them or more.
All inputs are finite; a program needn't handle non-finite values.
Results may differ from a plain program's by a relative error of at most 0.018.
Values may be sent and summed in bfloat16 or wider, within the bound.
No kernel may reach another device: no remote copies, remote signals or barrier semaphores. Data moves between devices by JAX's collectives and lax.ppermute only.
A program may use at most 256 MiB of HBM per device.

v0:
```python
import jax
import jax.numpy as jnp
from jax import lax
from jax.sharding import PartitionSpec as P

HEADS = 16
HEAD_DIM = 72
MICRO = 4


def normalize(values, gain, shift):
    centre = values - jnp.mean(values, axis=-1, keepdims=True)
    spread = jnp.mean(centre * centre, axis=-1, keepdims=True)
    return centre * lax.rsqrt(spread + 1e-06) * gain + shift


def gelu_tanh(values):
    return jax.nn.gelu(values, approximate=True)


def mat_rows(left, right):
    return lax.dot_general(
        left, right, (((0,), (0,)), ((), ())), preferred_element_type=jnp.float32
    )


def mat_last(left, right):
    return lax.dot_general(
        left, right, (((1,), (1,)), ((), ())), preferred_element_type=jnp.float32
    )


def score_block(query, all_kv, all_valid, width):
    images = all_kv.shape[0]
    seq_len = all_kv.shape[1]
    q_heads = query.reshape(images, -1, HEADS, HEAD_DIM)
    key_heads = all_kv[:, :, :width].reshape(images, seq_len, HEADS, HEAD_DIM)
    raw = jnp.einsum("iqhd,ikhd->ihqk", q_heads, key_heads, preferred_element_type=jnp.float32)
    raw = raw * HEAD_DIM ** (-0.5)
    return jnp.where(all_valid[:, None, None, :] > 0.5, raw, -1e30)


def per_device(
    patches,
    patch_mask,
    cotangent,
    w_qkv,
    w_out,
    w_up,
    w_down,
    gain_one,
    shift_one,
    gain_two,
    shift_two,
    bias_query,
    bias_value,
    bias_out,
    bias_up,
    bias_down,
):
    width = patches.shape[2]
    local_tokens = patches.shape[1]
    per_micro = patches.shape[0] // MICRO
    row_count = per_micro * local_tokens
    scale = HEAD_DIM ** (-0.5)
    row_parts = (
        lax.all_gather(w_qkv, "sa", axis=0, tiled=True),
        lax.all_gather(w_out, "sa", axis=0, tiled=True),
        lax.all_gather(w_up, "sa", axis=0, tiled=True),
        lax.all_gather(w_down, "sa", axis=0, tiled=True),
    )
    gathered = (
        lax.all_gather(row_parts[0], "dev", axis=1, tiled=True),
        lax.all_gather(row_parts[1], "dev", axis=1, tiled=True),
        lax.all_gather(row_parts[2], "dev", axis=1, tiled=True),
        lax.all_gather(row_parts[3], "dev", axis=1, tiled=True),
        lax.all_gather(gain_one, "dev", axis=1, tiled=True),
        lax.all_gather(shift_one, "dev", axis=1, tiled=True),
        lax.all_gather(gain_two, "dev", axis=1, tiled=True),
        lax.all_gather(shift_two, "dev", axis=1, tiled=True),
        lax.all_gather(bias_query, "dev", axis=1, tiled=True),
        lax.all_gather(bias_value, "dev", axis=1, tiled=True),
        lax.all_gather(bias_out, "dev", axis=1, tiled=True),
        lax.all_gather(bias_up, "dev", axis=1, tiled=True),
        lax.all_gather(bias_down, "dev", axis=1, tiled=True),
    )
    full_qkv, full_out, full_up, full_down = (gathered[0], gathered[1], gathered[2], gathered[3])
    vectors = [item.astype(jnp.float32)[0] for item in gathered[4:]]
    gain_first, shift_first, gain_second, shift_second = (
        vectors[0],
        vectors[1],
        vectors[2],
        vectors[3],
    )
    query_bias, value_bias, out_bias, up_bias, down_bias = (
        vectors[4],
        vectors[5],
        vectors[6],
        vectors[7],
        vectors[8],
    )
    qkv_bias = jnp.concatenate([query_bias, jnp.zeros((width,), jnp.float32), value_bias])
    outputs = []
    kept = []
    for micro_step in range(MICRO):
        begin = micro_step * per_micro
        inputs = patches[begin : begin + per_micro].astype(jnp.float32).reshape(row_count, width)
        normed_one = normalize(inputs, gain_first, shift_first).astype(jnp.bfloat16)
        projected = (
            jnp.dot(normed_one, full_qkv, preferred_element_type=jnp.float32) + qkv_bias
        ).astype(jnp.bfloat16)
        query = projected[:, :width]
        key_value = projected[:, width:].reshape(per_micro, local_tokens, 2 * width)
        valid = patch_mask[begin : begin + per_micro].astype(jnp.bfloat16)
        all_kv, all_valid = (
            lax.all_gather(key_value, "sa", axis=1, tiled=True),
            lax.all_gather(valid, "sa", axis=1, tiled=True),
        )
        seq_len = all_kv.shape[1]
        scores = score_block(query, all_kv, all_valid, width)
        peak = jnp.max(scores, axis=-1, keepdims=True)
        expo = jnp.exp(scores - peak)
        total = jnp.sum(expo, axis=-1, keepdims=True)
        log_total = peak + jnp.log(total)
        probs = (expo / total).astype(jnp.bfloat16)
        value_heads = all_kv[:, :, width:].reshape(per_micro, seq_len, HEADS, HEAD_DIM)
        attended = jnp.einsum(
            "ihqk,ikhd->iqhd", probs, value_heads, preferred_element_type=jnp.float32
        )
        attended = attended.reshape(row_count, width).astype(jnp.bfloat16)
        middle = inputs + jnp.dot(attended, full_out, preferred_element_type=jnp.float32) + out_bias
        normed_two = normalize(middle, gain_second, shift_second).astype(jnp.bfloat16)
        hidden_pre = jnp.dot(normed_two, full_up, preferred_element_type=jnp.float32) + up_bias
        activated = gelu_tanh(hidden_pre).astype(jnp.bfloat16)
        mlp_out = mat_last(activated, full_down) + down_bias
        outputs.append(
            (middle + mlp_out).astype(jnp.bfloat16).reshape(per_micro, local_tokens, width)
        )
        kept.append(
            (
                inputs,
                normed_one,
                query,
                key_value,
                valid,
                all_kv,
                all_valid,
                log_total,
                attended,
                middle,
                normed_two,
                hidden_pre,
                activated,
            )
        )
    rows_back = (
        lax.all_gather(w_qkv, "sa", axis=0, tiled=True),
        lax.all_gather(w_out, "sa", axis=0, tiled=True),
        lax.all_gather(w_up, "sa", axis=0, tiled=True),
        lax.all_gather(w_down, "sa", axis=0, tiled=True),
    )
    again = (
        lax.all_gather(rows_back[0], "dev", axis=1, tiled=True),
        lax.all_gather(rows_back[1], "dev", axis=1, tiled=True),
        lax.all_gather(rows_back[2], "dev", axis=1, tiled=True),
        lax.all_gather(rows_back[3], "dev", axis=1, tiled=True),
        lax.all_gather(gain_one, "dev", axis=1, tiled=True),
        lax.all_gather(shift_one, "dev", axis=1, tiled=True),
        lax.all_gather(gain_two, "dev", axis=1, tiled=True),
        lax.all_gather(shift_two, "dev", axis=1, tiled=True),
        lax.all_gather(bias_query, "dev", axis=1, tiled=True),
        lax.all_gather(bias_value, "dev", axis=1, tiled=True),
        lax.all_gather(bias_out, "dev", axis=1, tiled=True),
        lax.all_gather(bias_up, "dev", axis=1, tiled=True),
        lax.all_gather(bias_down, "dev", axis=1, tiled=True),
    )
    back_qkv, back_out, back_up, back_down = (again[0], again[1], again[2], again[3])
    back_vectors = [item.astype(jnp.float32)[0] for item in again[4:]]
    back_gain_first, back_shift_first = (back_vectors[0], back_vectors[1])
    back_gain_second, back_shift_second = (back_vectors[2], back_vectors[3])
    acc_qkv = jnp.zeros(back_qkv.shape, jnp.float32)
    acc_out = jnp.zeros(back_out.shape, jnp.float32)
    acc_up = jnp.zeros(back_up.shape, jnp.float32)
    acc_down = jnp.zeros(back_down.shape, jnp.float32)
    ff_width = back_up.shape[1]
    acc_vectors = [jnp.zeros((width,), jnp.float32) for index_value in range(7)] + [
        jnp.zeros((ff_width,), jnp.float32),
        jnp.zeros((width,), jnp.float32),
    ]
    grad_inputs = []
    for micro_step in range(MICRO):
        begin = micro_step * per_micro
        (
            inputs,
            normed_one,
            query,
            key_value,
            valid,
            all_kv,
            all_valid,
            log_total,
            attended,
            middle,
            normed_two,
            hidden_pre,
            activated,
        ) = kept[micro_step]
        seq_len = all_kv.shape[1]
        grad_out = (
            cotangent[begin : begin + per_micro].astype(jnp.float32).reshape(row_count, width)
        )
        grad_mlp = grad_out.astype(jnp.bfloat16)
        acc_down = acc_down + mat_rows(grad_mlp, activated)
        grad_act = jnp.dot(grad_mlp, back_down, preferred_element_type=jnp.float32)
        gelu_pull = jax.vjp(gelu_tanh, hidden_pre)[1]
        grad_hidden = gelu_pull(grad_act)[0].astype(jnp.bfloat16)
        acc_up = acc_up + mat_rows(normed_two, grad_hidden)
        grad_normed_two = mat_last(grad_hidden, back_up)
        norm_pull = jax.vjp(normalize, middle, back_gain_second, back_shift_second)[1]
        grad_middle_part, grad_gain_second, grad_shift_second = norm_pull(grad_normed_two)
        grad_middle = grad_out + grad_middle_part
        grad_branch = grad_middle.astype(jnp.bfloat16)
        acc_out = acc_out + mat_rows(attended, grad_branch)
        grad_att = mat_last(grad_branch, back_out).astype(jnp.bfloat16)
        grad_att_heads = grad_att.reshape(per_micro, local_tokens, HEADS, HEAD_DIM)
        scores = score_block(query, all_kv, all_valid, width)
        probs_full = jnp.exp(scores - log_total)
        probs = probs_full.astype(jnp.bfloat16)
        q_heads = query.reshape(per_micro, local_tokens, HEADS, HEAD_DIM)
        key_heads = all_kv[:, :, :width].reshape(per_micro, seq_len, HEADS, HEAD_DIM)
        value_heads = all_kv[:, :, width:].reshape(per_micro, seq_len, HEADS, HEAD_DIM)
        grad_probs = jnp.einsum(
            "iqhd,ikhd->ihqk", grad_att_heads, value_heads, preferred_element_type=jnp.float32
        )
        row_terms = jnp.sum(grad_probs * probs_full, axis=-1, keepdims=True)
        grad_scores = (probs_full * (grad_probs - row_terms)).astype(jnp.bfloat16)
        grad_query = (
            jnp.einsum(
                "ihqk,ikhd->iqhd", grad_scores, key_heads, preferred_element_type=jnp.float32
            )
            * scale
        )
        grad_value = jnp.einsum(
            "ihqk,iqhd->ikhd", probs, grad_att_heads, preferred_element_type=jnp.float32
        )
        grad_key = (
            jnp.einsum("ihqk,iqhd->ikhd", grad_scores, q_heads, preferred_element_type=jnp.float32)
            * scale
        )
        grad_kv_part = jnp.concatenate(
            [
                grad_key.reshape(per_micro, seq_len, width),
                grad_value.reshape(per_micro, seq_len, width),
            ],
            axis=2,
        )
        grad_kv = lax.psum_scatter(
            grad_kv_part.astype(jnp.bfloat16), "sa", scatter_dimension=1, tiled=True
        ).astype(jnp.float32)
        grad_proj = jnp.concatenate(
            [grad_query.reshape(row_count, width), grad_kv.reshape(row_count, 2 * width)], axis=1
        ).astype(jnp.bfloat16)
        acc_qkv = acc_qkv + mat_rows(normed_one, grad_proj)
        grad_normed_one = mat_last(grad_proj, back_qkv)
        first_pull = jax.vjp(normalize, inputs, back_gain_first, back_shift_first)[1]
        grad_in_part, grad_gain_first, grad_shift_first = first_pull(grad_normed_one)
        grad_inputs.append(
            (grad_middle + grad_in_part)
            .astype(jnp.bfloat16)
            .reshape(per_micro, local_tokens, width)
        )
        proj_sums = jnp.sum(grad_proj.astype(jnp.float32), axis=0)
        terms = [
            grad_gain_first,
            grad_shift_first,
            grad_gain_second,
            grad_shift_second,
            proj_sums[:width],
            proj_sums[2 * width :],
            jnp.sum(grad_branch.astype(jnp.float32), axis=0),
            jnp.sum(grad_hidden.astype(jnp.float32), axis=0),
            jnp.sum(grad_mlp.astype(jnp.float32), axis=0),
        ]
        acc_vectors = [held + fresh for held, fresh in zip(acc_vectors, terms)]
    row_sums = (
        lax.psum_scatter(
            acc_qkv.astype(jnp.bfloat16), "sa", scatter_dimension=0, tiled=True
        ).astype(jnp.float32),
        lax.psum_scatter(
            acc_out.astype(jnp.bfloat16), "sa", scatter_dimension=0, tiled=True
        ).astype(jnp.float32),
        lax.psum_scatter(acc_up.astype(jnp.bfloat16), "sa", scatter_dimension=0, tiled=True).astype(
            jnp.float32
        ),
        lax.psum_scatter(
            acc_down.astype(jnp.bfloat16), "sa", scatter_dimension=0, tiled=True
        ).astype(jnp.float32),
    )
    flat_vectors = [item[None, :] for item in acc_vectors]
    column_sums = (
        lax.psum_scatter(
            row_sums[0].astype(jnp.bfloat16), "dev", scatter_dimension=1, tiled=True
        ).astype(jnp.float32),
        lax.psum_scatter(
            row_sums[1].astype(jnp.bfloat16), "dev", scatter_dimension=1, tiled=True
        ).astype(jnp.float32),
        lax.psum_scatter(
            row_sums[2].astype(jnp.bfloat16), "dev", scatter_dimension=1, tiled=True
        ).astype(jnp.float32),
        lax.psum_scatter(
            row_sums[3].astype(jnp.bfloat16), "dev", scatter_dimension=1, tiled=True
        ).astype(jnp.float32),
        lax.psum_scatter(
            flat_vectors[0].astype(jnp.bfloat16), "dev", scatter_dimension=1, tiled=True
        ).astype(jnp.float32),
        lax.psum_scatter(
            flat_vectors[1].astype(jnp.bfloat16), "dev", scatter_dimension=1, tiled=True
        ).astype(jnp.float32),
        lax.psum_scatter(
            flat_vectors[2].astype(jnp.bfloat16), "dev", scatter_dimension=1, tiled=True
        ).astype(jnp.float32),
        lax.psum_scatter(
            flat_vectors[3].astype(jnp.bfloat16), "dev", scatter_dimension=1, tiled=True
        ).astype(jnp.float32),
        lax.psum_scatter(
            flat_vectors[4].astype(jnp.bfloat16), "dev", scatter_dimension=1, tiled=True
        ).astype(jnp.float32),
        lax.psum_scatter(
            flat_vectors[5].astype(jnp.bfloat16), "dev", scatter_dimension=1, tiled=True
        ).astype(jnp.float32),
        lax.psum_scatter(
            flat_vectors[6].astype(jnp.bfloat16), "dev", scatter_dimension=1, tiled=True
        ).astype(jnp.float32),
        lax.psum_scatter(
            flat_vectors[7].astype(jnp.bfloat16), "dev", scatter_dimension=1, tiled=True
        ).astype(jnp.float32),
        lax.psum_scatter(
            flat_vectors[8].astype(jnp.bfloat16), "dev", scatter_dimension=1, tiled=True
        ).astype(jnp.float32),
    )
    summed = lax.psum(
        (
            column_sums[4],
            column_sums[5],
            column_sums[6],
            column_sums[7],
            column_sums[8],
            column_sums[9],
            column_sums[10],
            column_sums[11],
            column_sums[12],
        ),
        "sa",
    )
    result = jnp.concatenate(outputs, axis=0)
    grad_patches = jnp.concatenate(grad_inputs, axis=0)
    return (
        result,
        grad_patches,
        column_sums[0],
        column_sums[1],
        column_sums[2],
        column_sums[3],
        summed[0],
        summed[1],
        summed[2],
        summed[3],
        summed[4],
        summed[5],
        summed[6],
        summed[7],
        summed[8],
    )


def solution(mesh):
    placed = (
        P("dev", "sa", None),
        P("dev", "sa"),
        P("dev", "sa", None),
        P("sa", "dev"),
        P("sa", "dev"),
        P("sa", "dev"),
        P("sa", "dev"),
        P(None, "dev"),
        P(None, "dev"),
        P(None, "dev"),
        P(None, "dev"),
        P(None, "dev"),
        P(None, "dev"),
        P(None, "dev"),
        P(None, "dev"),
        P(None, "dev"),
    )
    return jax.shard_map(
        per_device,
        mesh=mesh,
        in_specs=placed,
        out_specs=(
            P("dev", "sa", None),
            P("dev", "sa", None),
            P("sa", "dev"),
            P("sa", "dev"),
            P("sa", "dev"),
            P("sa", "dev"),
            P(None, "dev"),
            P(None, "dev"),
            P(None, "dev"),
            P(None, "dev"),
            P(None, "dev"),
            P(None, "dev"),
            P(None, "dev"),
            P(None, "dev"),
            P(None, "dev"),
        ),
        check_vma=False,
    )
```

profile of v0, /device:TPU:0, one launch (start us, length us, event | category | flops | bytes accessed | tf_op | source)
XLA Modules:
  0.0 1915.4 jit_solution(13595690874956938875)
XLA Ops:
  8.0 55.3 %all-gather.17.cloned.1.call-done = bf16[1152,1728]{1,0:T(8,128)(2,1)} async-done(((bf16[72,1728]{1,0:T(8,128)(2,1)}), bf16[1152,1728]{1,0:T(8,128)(2,1)}) %all-gather.17.cloned.1.call-update) | async-done | bytes 3981328 | tf_op jit(solution)/shard_map/all_gather | solution.py:67
  63.3 6.5 copy.142
  75.8 8.9 all-reduce.21
  85.8 82.3 %all-gather.19.cloned.1.call-done = bf16[1152,3456]{0,1:T(8,128)(2,1)} async-done(((bf16[1152,1728]{0,1:T(8,128)(2,1)}), bf16[1152,3456]{0,1:T(8,128)(2,1)}) %all-gather.19.cloned.1.call-update) | async-done | bytes 7962640 | tf_op jit(solution)/shard_map/all_gather | solution.py:73
  174.8 5.8 fusion.7
  181.5 5.8 fusion.8
  188.1 21.2 %all-gather.21.cloned.1.call-done = bf16[1152,576]{1,0:T(8,128)(2,1)} async-done(((bf16[72,576]{1,0:T(8,128)(2,1)}), bf16[1152,576]{1,0:T(8,128)(2,1)}) %all-gather.21.cloned.1.call-update) | async-done | bytes 1327120 | tf_op jit(solution)/shard_map/all_gather | solution.py:68
  211.9 53.1 %all-gather.25.cloned.1.call-done = bf16[1152,2152]{1,0:T(8,128)(2,1)} async-done(((bf16[72,2152]{1,0:T(8,128)(2,1)}), bf16[1152,2152]{1,0:T(8,128)(2,1)}) %all-gather.25.cloned.1.call-update) | async-done | bytes 4958224 | tf_op jit(solution)/shard_map/all_gather | solution.py:69
  265.0 8.5 copy.148
  277.5 32.7 %all-reduce.19 = (bf16[1024]{0:T(1024)(128)(2,1)S(1)}, bf16[1024]{0:T(1024)(128)(2,1)S(1)}, bf16[1024]{0:T(1024)(128)(2,1)S(1)}, bf16[1024]{0:T(1024)(128)(2,1)S(1)}) all-reduce(bf16[1024]{0:T(1024)(128)(2,1)S(1)} %dynamic-update-slice.10, bf16[1024]{0:T(1024)(128)(2,1)S(1)} %dynamic-update-slice.12, ...), channel_id=1, replica_groups=mesh['dev'=2,'sa'=16] {'sa'}, use_global_device_ids=true, to_apply=%add.10 | all-reduce | flops 4096 | bytes 16384
  310.8 10.2 all-gather.29.cloned.1.call-done
  321.0 8.4 copy.149
  332.0 44.0 %all-gather.35.cloned.1.call-done = bf16[1024,2304]{1,0:T(8,128)(2,1)} async-done(((bf16[64,2304]{1,0:T(8,128)(2,1)}), bf16[1024,2304]{1,0:T(8,128)(2,1)}) %all-gather.35.cloned.1.call-update) | async-done | bytes 4718608 | tf_op jit(solution)/shard_map/all_gather | solution.py:116
  382.7 48.1 %all-gather.37.cloned.1.call-done = bf16[1024,2304]{1,0:T(8,128)(2,1)} async-done(((bf16[64,2304]{1,0:T(8,128)(2,1)}), bf16[1024,2304]{1,0:T(8,128)(2,1)}) %all-gather.37.cloned.1.call-update) | async-done | bytes 4718608 | tf_op jit(solution)/shard_map/all_gather | solution.py:116
  438.5 47.1 %all-gather.39.cloned.1.call-done = bf16[1024,2304]{1,0:T(8,128)(2,1)} async-done(((bf16[64,2304]{1,0:T(8,128)(2,1)}), bf16[1024,2304]{1,0:T(8,128)(2,1)}) %all-gather.39.cloned.1.call-update) | async-done | bytes 4718608 | tf_op jit(solution)/shard_map/all_gather | solution.py:116
  543.8 106.0 %all-gather.27.cloned.1.call-done = bf16[1152,4304]{0,1:T(8,128)(2,1)} async-done(((bf16[1152,2152]{0,1:T(8,128)(2,1)}), bf16[1152,4304]{0,1:T(8,128)(2,1)}) %all-gather.27.cloned.1.call-update) | async-done | bytes 9916432 | tf_op jit(solution)/shard_map/all_gather | solution.py:75
  649.9 16.5 convolution_add_fusion.14
  666.4 108.3 %all-gather.31.cloned.1.call-done = bf16[1152,4304]{0,1:T(8,128)(2,1)} async-done(((bf16[1152,2152]{0,1:T(8,128)(2,1)}), bf16[1152,4304]{0,1:T(8,128)(2,1)}) %all-gather.31.cloned.1.call-update) | async-done | bytes 9916432 | tf_op jit(solution)/shard_map/all_gather | solution.py:76
  774.8 7.9 convert_reduce_fusion.6
  790.2 5.8 convert_reduce_fusion.4
  803.7 6.0 convert_reduce_fusion.5
  829.9 21.4 %copy.189 = bf16[1,1024,2304]{2,0,1:T(2,128)(2,1)} copy(bf16[1,1024,2304]{1,2,0:T(8,128)(2,1)} %pad_maximum_fusion.1) | data formatting | bytes 9437184
  851.3 6.6 copy.283
  871.4 21.5 %copy.193 = bf16[1,1024,2304]{2,0,1:T(2,128)(2,1)} copy(bf16[1,1024,2304]{1,2,0:T(8,128)(2,1)} %pad_maximum_fusion.3) | data formatting | bytes 9437184
  892.9 6.6 copy.281
  912.9 21.5 %copy.191 = bf16[1,1024,2304]{2,0,1:T(2,128)(2,1)} copy(bf16[1,1024,2304]{1,2,0:T(8,128)(2,1)} %pad_maximum_fusion.2) | data formatting | bytes 9437184
  934.4 6.5 copy.282
  963.3 49.4 %reduce-scatter.66.cloned.1.call-done = bf16[64,2304]{1,0:T(8,128)(2,1)} async-done(((bf16[1024,2304]{1,0:T(8,128)(2,1)}), bf16[64,2304]{1,0:T(8,128)(2,1)}) %reduce-scatter.66.cloned.1.call-update) | async-done | bytes 294928
  1016.8 74.2 %reduce-scatter.64.cloned.1.call-done = bf16[64,2304]{1,0:T(8,128)(2,1)} async-done(((bf16[1024,2304]{1,0:T(8,128)(2,1)}), bf16[64,2304]{1,0:T(8,128)(2,1)}) %reduce-scatter.64.cloned.1.call-update) | async-done | bytes 294928
  1115.5 49.6 %all-gather.33.cloned.1.call-done = bf16[1024,2304]{1,0:T(8,128)(2,1)} async-done(((bf16[64,2304]{1,0:T(8,128)(2,1)}), bf16[1024,2304]{1,0:T(8,128)(2,1)}) %all-gather.33.cloned.1.call-update) | async-done | bytes 4718608 | tf_op jit(solution)/shard_map/all_gather | solution.py:116
  1189.1 7.0 convolution_add_fusion.15
  1196.1 7.9 convert_reduce_fusion.7
  1225.3 21.5 %copy.187 = bf16[1,1024,2304]{2,0,1:T(2,128)(2,1)} copy(bf16[1,1024,2304]{1,2,0:T(8,128)(2,1)} %pad_maximum_fusion) | data formatting | bytes 9437184
  1246.9 6.7 copy.284
  1255.4 8.5 fusion.245
  1264.0 12.9 convolution_add_fusion.5
  1277.0 13.4 convolution_add_fusion.4
  1290.3 13.4 fusion
  1305.4 8.4 fusion.201
  1313.9 12.6 convolution_add_fusion.2
  1328.8 12.8 convolution_add_fusion.1
  1343.4 14.0 fusion.2
  1357.5 14.1 copy.201
  1381.9 11.2 fusion.156
  1393.1 8.7 convolution_add_fusion.8
  1401.9 8.2 convolution_add_fusion.7
  1410.1 11.2 fusion.3
  1433.4 9.1 all-reduce.20
  1442.5 6.7 fusion.30
  1449.2 6.6 fusion.31
  1463.9 6.7 fusion.32
  1470.5 18.1 reduce-scatter.58.cloned.1.call-done
  1488.8 5.8 fusion.29
  1503.6 12.8 reduce-scatter.78.cloned.1.call-done
  1518.0 12.8 reduce-scatter.80.cloned.1.call-done
  1532.4 12.8 reduce-scatter.70.cloned.1.call-done
  1546.9 119.3 %reduce-scatter.72.cloned.1.call-done = bf16[72,4304]{1,0:T(8,128)(2,1)} async-done(((bf16[1152,4304]{1,0:T(8,128)(2,1)}), bf16[72,4304]{1,0:T(8,128)(2,1)}) %reduce-scatter.72.cloned.1.call-update) | async-done | bytes 619792
  1674.3 96.4 %reduce-scatter.90.cloned.1.call-done = bf16[72,3456]{1,0:T(8,128)(2,1)} async-done(((bf16[1152,3456]{1,0:T(8,128)(2,1)}), bf16[72,3456]{1,0:T(8,128)(2,1)}) %reduce-scatter.90.cloned.1.call-update) | async-done | bytes 497680
  1775.0 10.2 reduce-scatter.74.cloned.1.call-done
  1786.3 13.7 reduce-scatter.76.cloned.1.call-done
  1801.0 13.3 reduce-scatter.84.cloned.1.call-done
  1815.3 13.3 reduce-scatter.82.cloned.1.call-done
  1829.7 63.4 %all-reduce.18 = (f32[1,576]{1,0:T(1,128)}, f32[1,576]{1,0:T(1,128)}, f32[1,576]{1,0:T(1,128)}, f32[1,576]{1,0:T(1,128)}, f32[1,576]{1,0:T(1,128)}, /*index=5*/f...) all-reduce(bf16[1,576]{1,0:T(2,128)(2,1)S(1)} %copy.204, ...), channel_id=1, replica_groups=mesh['dev'=2,'sa'=16] {'sa'}, use_global_device_ids=true, to_apply=%region_61.62 | all-reduce | flops 6760 | bytes 44864 | tf_op jit(solution)/shard_map/psum | solution.py:341
  1897.2 9.2 reduce-scatter.68.cloned.1.call-done
  (820 shorter events, 326.3 us)
Async XLA Ops:
  7.2 56.1 %all-gather.17.cloned.1.call-start = ((), (), s32[]{:S(2)}) async-start(), calls=%async_computation.19 | async-start | bytes 4386816 | tf_op jit(solution)/shard_map/all_gather | solution.py:67
  7.9 160.2 %all-gather.19.cloned.1.call-start = ((), (), s32[]{:S(2)}) async-start(), calls=%async_computation.20 | async-start | bytes 11943936 | tf_op jit(solution)/shard_map/all_gather | solution.py:73
  69.9 139.4 %all-gather.21.cloned.1.call-start = ((), (), s32[]{:S(2)}) async-start(), calls=%async_computation.21 | async-start | bytes 1566720 | tf_op jit(solution)/shard_map/all_gather | solution.py:68
  70.6 194.4 %all-gather.25.cloned.1.call-start = ((), (), s32[]{:S(2)}) async-start(), calls=%async_computation.23 | async-start | bytes 5326848 | tf_op jit(solution)/shard_map/all_gather | solution.py:69
  71.2 249.9 %all-gather.29.cloned.1.call-start = ((), (), s32[]{:S(2)}) async-start(), calls=%async_computation.25 | async-start | bytes 5326848 | tf_op jit(solution)/shard_map/all_gather | solution.py:70
  71.8 304.2 %all-gather.35.cloned.1.call-start = ((), (), s32[]{:S(2)}) async-start(), calls=%async_computation.29 | async-start | bytes 5013504 | tf_op jit(solution)/shard_map/all_gather | solution.py:116
  84.7 96.7 %copy-start.85 = (f32[1152]{0:T(1024)}, f32[1152]{0:T(1024)S(1)}, u32[]{:S(2)}) copy-start(f32[1152]{0:T(1024)S(1)} %mul.941) | copy-start | bytes 13828
  84.7 96.7 %copy-start.102 = (f32[1152]{0:T(1024)}, f32[1152]{0:T(1024)S(1)}, u32[]{:S(2)}) copy-start(f32[1152]{0:T(1024)S(1)} %add.879) | copy-start | bytes 13828
  84.8 96.6 %copy-start.111 = (f32[3456]{0:T(1024)}, f32[3456]{0:T(1024)S(1)}, u32[]{:S(2)}) copy-start(f32[3456]{0:T(1024)S(1)} %pad_maximum_fusion.18) | copy-start | bytes 41476
  85.5 89.3 %copy-start.158 = (f32[64]{0:T(128)}, f32[64]{0:T(128)S(1)}, u32[]{:S(2)}) copy-start(f32[64]{0:T(128)S(1)} %broadcast_multiply_fusion.3) | copy-start | bytes 772
  85.5 88.4 %copy-start.150 = (f32[64]{0:T(128)}, f32[64]{0:T(128)S(1)}, u32[]{:S(2)}) copy-start(f32[64]{0:T(128)S(1)} %get-tuple-element.231) | copy-start | bytes 772
  85.5 96.0 %copy-start.153 = (f32[64]{0:T(128)}, f32[64]{0:T(128)S(1)}, u32[]{:S(2)}) copy-start(f32[64]{0:T(128)S(1)} %get-tuple-element.230) | copy-start | bytes 772
  85.8 88.1 %copy-start.223 = (f32[64]{0:T(128)}, f32[64]{0:T(128)S(1)}, u32[]{:S(2)}) copy-start(f32[64]{0:T(128)S(1)} %get-tuple-element.108) | copy-start | bytes 772
  85.8 88.9 %copy-start.225 = (f32[64]{0:T(128)}, f32[64]{0:T(128)S(1)}, u32[]{:S(2)}) copy-start(f32[64]{0:T(128)S(1)} %get-tuple-element.110) | copy-start | bytes 772
  85.8 95.6 %copy-start.221 = (f32[64]{0:T(128)}, f32[64]{0:T(128)S(1)}, u32[]{:S(2)}) copy-start(f32[64]{0:T(128)S(1)} %get-tuple-element.109) | copy-start | bytes 772
  85.8 88.1 %copy-start.188 = (f32[64]{0:T(128)}, f32[64]{0:T(128)S(1)}, u32[]{:S(2)}) copy-start(f32[64]{0:T(128)S(1)} %fusion.219) | copy-start | bytes 772
  174.7 256.1 %all-gather.37.cloned.1.call-start = ((), (), s32[]{:S(2)}) async-start(), calls=%async_computation.30 | async-start | bytes 5013504 | tf_op jit(solution)/shard_map/all_gather | solution.py:116
  181.4 304.3 %all-gather.39.cloned.1.call-start = ((), (), s32[]{:S(2)}) async-start(), calls=%async_computation.31 | async-start | bytes 5013504 | tf_op jit(solution)/shard_map/all_gather | solution.py:116
  188.0 344.5 %all-gather.23.cloned.1.call-start = ((), (), s32[]{:S(2)}) async-start(), calls=%async_computation.22 | async-start | bytes 3981312 | tf_op jit(solution)/shard_map/all_gather | solution.py:74
  211.9 438.0 %all-gather.27.cloned.1.call-start = ((), (), s32[]{:S(2)}) async-start(), calls=%async_computation.24 | async-start | bytes 14874624 | tf_op jit(solution)/shard_map/all_gather | solution.py:75
  273.6 501.2 %all-gather.31.cloned.1.call-start = ((), (), s32[]{:S(2)}) async-start(), calls=%async_computation.26 | async-start | bytes 14874624 | tf_op jit(solution)/shard_map/all_gather | solution.py:76
  329.5 629.6 %reduce-scatter.62.cloned.1.call-start = ((), (), s32[]{:S(2)}) async-start(), calls=%async_computation.33 | async-start | bytes 5013504
  331.5 194.5 %copy-start.78 = (bf16[64,16,72]{2,1,0:T(8,128)(2,1)}, bf16[64,16,72]{2,1,0:T(8,128)(2,1)S(1)}, u32[]{:S(2)}) copy-start(bf16[64,16,72]{2,1,0:T(8,128)(2,1)S(1)} %reshape.1191) | copy-start | bytes 442372
  332.0 185.9 %copy-start.80 = (bf16[64,16,72]{2,1,0:T(8,128)(2,1)}, bf16[64,16,72]{2,1,0:T(8,128)(2,1)S(1)}, u32[]{:S(2)}) copy-start(bf16[64,16,72]{2,1,0:T(8,128)(2,1)S(1)} %reshape.1197) | copy-start | bytes 442372
  438.5 87.5 %copy-start.14 = (bf16[1,1024,1152]{1,2,0:T(8,128)(2,1)}, bf16[1,1024,1152]{1,2,0:T(8,128)(2,1)S(1)}, u32[]{:S(2)}) copy-start(bf16[1,1024,1152]{1,2,0:T(8,128)(2,1)S(1)} %copy.155) | copy-start | bytes 7077892
  535.9 277.8 %copy-start.19 = (f32[64,1152]{1,0:T(8,128)}, f32[64,1152]{1,0:T(8,128)S(1)}, u32[]{:S(2)}) copy-start(f32[64,1152]{1,0:T(8,128)S(1)} %get-tuple-element.209) | copy-start | bytes 884740
  858.0 154.7 %reduce-scatter.66.cloned.1.call-start = ((), (), s32[]{:S(2)}) async-start(), calls=%async_computation.35 | async-start | bytes 5013504
  899.5 191.5 %reduce-scatter.64.cloned.1.call-start = ((), (), s32[]{:S(2)}) async-start(), calls=%async_computation.34 | async-start | bytes 5013504
  941.0 224.0 %all-gather.33.cloned.1.call-start = ((), (), s32[]{:S(2)}) async-start(), calls=%async_computation.28 | async-start | bytes 5013504 | tf_op jit(solution)/shard_map/all_gather | solution.py:116
  947.3 153.0 %copy-start.48 = (bf16[1,64,16,72]{1,3,2,0:T(8,128)(2,1)}, bf16[1,64,16,72]{1,3,2,0:T(8,128)(2,1)S(1)}, u32[]{:S(2)}) copy-start(bf16[1,64,16,72]{1,3,2,0:T(8,128)(2,1)S(1)} %copy.185) | copy-start | bytes 442372
  1112.4 229.1 %reduce-scatter.92.cloned.1.call-start = ((), (), s32[]{:S(2)}) async-start(), calls=%async_computation.49 | async-start | bytes 2820096
  1115.4 63.2 %copy-start.83 = (bf16[64,16,72]{2,1,0:T(8,128)(2,1)}, bf16[64,16,72]{2,1,0:T(8,128)(2,1)S(1)}, u32[]{:S(2)}) copy-start(bf16[64,16,72]{2,1,0:T(8,128)(2,1)S(1)} %reshape.1179) | copy-start | bytes 442372
  1188.8 66.5 %copy-start.28 = (f32[64,1152]{1,0:T(8,128)}, f32[64,1152]{1,0:T(8,128)S(1)}, u32[]{:S(2)}) copy-start(f32[64,1152]{1,0:T(8,128)S(1)} %get-tuple-element.221) | copy-start | bytes 884740
  1213.5 164.1 %reduce-scatter.60.cloned.1.call-start = ((), (), s32[]{:S(2)}) async-start(), calls=%async_computation.32 | async-start | bytes 5013504
  1253.6 169.4 %reduce-scatter.88.cloned.1.call-start = ((), (), s32[]{:S(2)}) async-start(), calls=%async_computation.46 | async-start | bytes 442368
  1255.3 233.4 %reduce-scatter.58.cloned.1.call-start = ((), (), s32[]{:S(2)}) async-start(), calls=%async_computation.27 | async-start | bytes 10653696 | tf_op jit(solution)/shard_map/reduce_scatter | solution.py:292
  1303.8 198.2 %reduce-scatter.86.cloned.1.call-start = ((), (), s32[]{:S(2)}) async-start(), calls=%async_computation.45 | async-start | bytes 442368
  1326.5 189.8 %reduce-scatter.78.cloned.1.call-start = ((), (), s32[]{:S(2)}) async-start(), calls=%async_computation.41 | async-start | bytes 442368
  1327.6 203.1 %reduce-scatter.80.cloned.1.call-start = ((), (), s32[]{:S(2)}) async-start(), calls=%async_computation.42 | async-start | bytes 442368
  1328.7 216.5 %reduce-scatter.70.cloned.1.call-start = ((), (), s32[]{:S(2)}) async-start(), calls=%async_computation.37 | async-start | bytes 442368
  1343.4 322.8 %reduce-scatter.72.cloned.1.call-start = ((), (), s32[]{:S(2)}) async-start(), calls=%async_computation.38 | async-start | bytes 10653696
  1371.6 399.1 %reduce-scatter.90.cloned.1.call-start = ((), (), s32[]{:S(2)}) async-start(), calls=%async_computation.48 | async-start | bytes 8460288
  1421.4 363.8 %reduce-scatter.74.cloned.1.call-start = ((), (), s32[]{:S(2)}) async-start(), calls=%async_computation.39 | async-start | bytes 442368
  1461.1 338.9 %reduce-scatter.76.cloned.1.call-start = ((), (), s32[]{:S(2)}) async-start(), calls=%async_computation.40 | async-start | bytes 442368
  1461.7 352.6 %reduce-scatter.84.cloned.1.call-start = ((), (), s32[]{:S(2)}) async-start(), calls=%async_computation.44 | async-start | bytes 442368
  1462.8 365.8 %reduce-scatter.82.cloned.1.call-start = ((), (), s32[]{:S(2)}) async-start(), calls=%async_computation.43 | async-start | bytes 442368
  1463.8 429.3 %all-reduce.24.cloned.1.call-start = ((), (), s32[]{:S(2)}) async-start(), calls=%async_computation.47 | async-start | bytes 1253376
  1488.7 406.3 %reduce-scatter.94.cloned.1.call-start = ((), (), s32[]{:S(2)}) async-start(), calls=%async_computation.50 | async-start | bytes 1652736
  1494.6 177.9 %copy-start.47 = (bf16[4,64,1152]{2,1,0:T(8,128)(2,1)S(1)}, bf16[4,64,1152]{2,1,0:T(8,128)(2,1)}, u32[]{:S(2)}) copy-start(bf16[4,64,1152]{2,1,0:T(8,128)(2,1)} %param.18) | copy-start | bytes 1769476
  1494.6 177.9 %copy-start.53 = (f32[64,1152]{1,0:T(8,128)S(1)}, f32[64,1152]{1,0:T(8,128)}, u32[]{:S(2)}) copy-start(f32[64,1152]{1,0:T(8,128)} %copy-done.51) | copy-start | bytes 884740
  1494.7 177.9 %copy-start.57 = (f32[64,1152]{1,0:T(8,128)S(1)}, f32[64,1152]{1,0:T(8,128)}, u32[]{:S(2)}) copy-start(f32[64,1152]{1,0:T(8,128)} %copy-done.55) | copy-start | bytes 884740
  1494.7 177.9 %copy-start.67 = (f32[64,1152]{1,0:T(8,128)S(1)}, f32[64,1152]{1,0:T(8,128)}, u32[]{:S(2)}) copy-start(f32[64,1152]{1,0:T(8,128)} %copy-done.66) | copy-start | bytes 884740
  1494.7 177.9 %copy-start.69 = (f32[64,1152]{1,0:T(8,128)S(1)}, f32[64,1152]{1,0:T(8,128)}, u32[]{:S(2)}) copy-start(f32[64,1152]{1,0:T(8,128)} %copy-done.68) | copy-start | bytes 884740
  1668.5 104.5 %copy-start.65 = (f32[64,1152]{1,0:T(8,128)S(1)}, f32[64,1152]{1,0:T(8,128)}, u32[]{:S(2)}) copy-start(f32[64,1152]{1,0:T(8,128)} %copy-done.64) | copy-start | bytes 884740
  1668.5 104.5 %copy-start.71 = (f32[64,1152]{1,0:T(8,128)S(1)}, f32[64,1152]{1,0:T(8,128)}, u32[]{:S(2)}) copy-start(f32[64,1152]{1,0:T(8,128)} %copy-done.70) | copy-start | bytes 884740
  1668.5 104.5 %copy-start.73 = (f32[64,1152]{1,0:T(8,128)S(1)}, f32[64,1152]{1,0:T(8,128)}, u32[]{:S(2)}) copy-start(f32[64,1152]{1,0:T(8,128)} %copy-done.72) | copy-start | bytes 884740
  1668.5 104.5 %copy-start.75 = (f32[64,1152]{1,0:T(8,128)S(1)}, f32[64,1152]{1,0:T(8,128)}, u32[]{:S(2)}) copy-start(f32[64,1152]{1,0:T(8,128)} %get-tuple-element.217) | copy-start | bytes 884740
  1668.5 237.8 %reduce-scatter.68.cloned.1.call-start = ((), (), s32[]{:S(2)}) async-start(), calls=%async_computation.36 | async-start | bytes 1327104
  1674.3 99.8 %copy-start.105 = (bf16[1,64,1152]{2,1,0:T(8,128)(2,1)S(1)}, bf16[1,64,1152]{2,1,0:T(8,128)(2,1)}, u32[]{:S(2)}) copy-start(bf16[1,64,1152]{2,1,0:T(8,128)(2,1)} %get-tuple-element.168) | copy-start | bytes 442372
  1674.3 99.8 %copy-start.106 = (bf16[1,64,1152]{2,1,0:T(8,128)(2,1)S(1)}, bf16[1,64,1152]{2,1,0:T(8,128)(2,1)}, u32[]{:S(2)}) copy-start(bf16[1,64,1152]{2,1,0:T(8,128)(2,1)} %get-tuple-element.169) | copy-start | bytes 442372
  1773.0 56.6 %copy-start.191 = (bf16[1,576]{1,0:T(2,128)(2,1)S(1)}, bf16[1,576]{1,0:T(2,128)(2,1)}, u32[]{:S(2)}) copy-start(bf16[1,576]{1,0:T(2,128)(2,1)} %copy.220) | copy-start | bytes 3460
  1773.0 56.6 %copy-start.192 = (bf16[1,576]{1,0:T(2,128)(2,1)S(1)}, bf16[1,576]{1,0:T(2,128)(2,1)}, u32[]{:S(2)}) copy-start(bf16[1,576]{1,0:T(2,128)(2,1)} %copy.216) | copy-start | bytes 3460
  1773.0 56.6 %copy-start.193 = (bf16[1,576]{1,0:T(2,128)(2,1)S(1)}, bf16[1,576]{1,0:T(2,128)(2,1)}, u32[]{:S(2)}) copy-start(bf16[1,576]{1,0:T(2,128)(2,1)} %copy.208) | copy-start | bytes 3460
  1773.0 56.6 %copy-start.194 = (bf16[1,576]{1,0:T(2,128)(2,1)S(1)}, bf16[1,576]{1,0:T(2,128)(2,1)}, u32[]{:S(2)}) copy-start(bf16[1,576]{1,0:T(2,128)(2,1)} %copy.210) | copy-start | bytes 3460
  (215 other events, 1192.5 us)
Sparse Core Ops, SparseCore 0:
  10.3 52.9 all-gather.16
  70.0 98.0 all-gather.18
  170.3 38.9 all-gather.20
  211.3 53.7 all-gather.24
  267.0 53.9 all-gather.28
  323.8 52.1 all-gather.34
  378.8 51.9 all-gather.36
  433.6 51.9 all-gather.38
  487.2 37.9 all-gather.22
  526.5 123.3 all-gather.26
  651.5 123.2 all-gather.30
  858.1 75.5 reduce-scatter.61
  938.0 74.6 reduce-scatter.65
  1016.4 74.5 reduce-scatter.63
  1112.6 52.4 all-gather.32
  1213.6 62.4 reduce-scatter.91
  1279.8 74.4 reduce-scatter.59
  1356.4 11.0 reduce-scatter.87
  1372.2 116.4 reduce-scatter.57
  1490.8 11.0 reduce-scatter.85
  1504.3 12.0 reduce-scatter.77
  1518.7 12.0 reduce-scatter.79
  1533.1 12.0 reduce-scatter.69
  1549.8 116.4 reduce-scatter.71
  1670.8 99.8 reduce-scatter.89
  1773.4 11.8 reduce-scatter.73
  1787.9 12.0 reduce-scatter.75
  1802.2 12.0 reduce-scatter.83
  1816.5 12.0 reduce-scatter.81
  1830.8 30.8 all-reduce.23
  1863.9 21.4 reduce-scatter.93
  1887.8 18.5 reduce-scatter.67
where the time goes:
time: 1930 us; the launch traced here: 1920 us
  waiting for transfers between devices  1090 us (56%)
  matrix products  339 us (18%)
  local copies, waits for them, and re-layouts  299 us (15%)
  blocking collectives  114 us (6%)
  other arithmetic  49.7 us (3%)
  between operations  20.6 us (1%)
    unnamed x51, waiting for transfers between devices  446 us
    unnamed x562, local copies, waits for them, and re-layouts  197 us
    all_gather x4, waiting for transfers between devices, per_device(): lax.all_gather(key_value, 'sa', axis=1, tiled=True)  189 us
    dot_general x16, matrix products, mat_rows(): lax.dot_general(left, right, (((0,), (0,)), ((), ())), preferred_element_...  140 us
    all_gather x1, waiting for transfers between devices, per_device(): lax.all_gather(row_parts[3], 'dev', axis=1, tiled=True)  108 us
    all_gather x1, waiting for transfers between devices, per_device(): lax.all_gather(row_parts[2], 'dev', axis=1, tiled=True)  106 us
    all_gather x1, waiting for transfers between devices, per_device(): lax.all_gather(row_parts[0], 'dev', axis=1, tiled=True)  82.3 us
    psum x1, blocking collectives, per_device(): lax.psum((column_sums[4], column_sums[5], column_sums[6], column_sums[7],...  63.4 us
  transfers between devices with their start and end apart: 32, of which 25 were waited for; matrix products, arithmetic and copies ran while one was open for 27% of the time, Pallas kernels for 0%

commit v1 on v0

--- a/solution.py
+++ b/solution.py
@@ -6,6 +6,18 @@
 HEADS = 16
 HEAD_DIM = 72
 MICRO = 4
+
+
+def gather_by_bits(shard, axis, dim):
+    ways, here = (lax.axis_size(axis), lax.axis_index(axis))
+    grown, reach = (shard, 1)
+    while reach < ways:
+        theirs = lax.ppermute(grown, axis, [(d, d ^ reach) for d in range(ways)])
+        mine_first = jnp.concatenate([grown, theirs], axis=dim)
+        theirs_first = jnp.concatenate([theirs, grown], axis=dim)
+        grown = jnp.where(here & reach == 0, mine_first, theirs_first)
+        reach = 2 * reach
+    return grown
 
 
 def normalize(values, gain, shift):
@@ -64,7 +76,7 @@
     row_count = per_micro * local_tokens
     scale = HEAD_DIM ** (-0.5)
     row_parts = (
-        lax.all_gather(w_qkv, "sa", axis=0, tiled=True),
+        gather_by_bits(w_qkv, "sa", 0),
         lax.all_gather(w_out, "sa", axis=0, tiled=True),
         lax.all_gather(w_up, "sa", axis=0, tiled=True),
         lax.all_gather(w_down, "sa", axis=0, tiled=True),

time: 1930 us -> 2110 us (1.093)
  waiting for transfers between devices: 1090 us -> 1260 us
    ppermute x0 -> x4, waiting for transfers between devices: none -> 124 us  [gather_by_bits(): theirs = lax.ppermute(grown, axis, [(d, d ^ reach) for d in range(ways)])]
    all_gather x0 -> x1, waiting for transfers between devices: none -> 95.6 us  [per_device(): lax.all_gather(rows_back[0], 'dev', axis=1, tiled=True)]
    all_gather x1, waiting for transfers between devices: 55.3 us -> 0.02 us  [per_device(): lax.all_gather(w_qkv, 'sa', axis=0, tiled=True)]
    all_gather x4, waiting for transfers between devices: 189 us -> 142 us  [per_device(): lax.all_gather(key_value, 'sa', axis=1, tiled=True)]
    all_gather x1, waiting for transfers between devices: 10.2 us -> 47 us  [per_device(): lax.all_gather(w_down, 'sa', axis=0, tiled=True)]
    unnamed x51 -> x52, waiting for transfers between devices: 446 us -> 440 us
    unnamed x562 -> x552, local copies, waits for them, and re-layouts: 197 us -> 199 us
  transfers between devices with their start and end apart: 32 -> 37, of which waited for: 25 -> 30; matrix products, arithmetic and copies ran while one was open for 27% -> 29% of each run, Pallas kernels for 0% -> 0%
where the time goes in v1:
time: 2110 us; the launch traced here: 2100 us
  waiting for transfers between devices  1260 us (60%)
  matrix products  330 us (16%)
  local copies, waits for them, and re-layouts  309 us (15%)
  blocking collectives  113 us (5%)
  other arithmetic  57.4 us (3%)
    unnamed x52, waiting for transfers between devices  440 us
    unnamed x552, local copies, waits for them, and re-layouts  199 us
    all_gather x4, waiting for transfers between devices, per_device(): lax.all_gather(key_value, 'sa', axis=1, tiled=True)  142 us
    dot_general x16, matrix products, mat_rows(): lax.dot_general(left, right, (((0,), (0,)), ((), ())), preferred_element_...  141 us
    ppermute x4, waiting for transfers between devices, gather_by_bits(): theirs = lax.ppermute(grown, axis, [(d, d ^ reach) for d in range(ways)])  124 us
    all_gather x1, waiting for transfers between devices, per_device(): lax.all_gather(row_parts[3], 'dev', axis=1, tiled=True)  117 us
    all_gather x1, waiting for transfers between devices, per_device(): lax.all_gather(rows_back[0], 'dev', axis=1, tiled=True)  95.6 us
    all_gather x1, waiting for transfers between devices, per_device(): lax.all_gather(row_parts[2], 'dev', axis=1, tiled=True)  94.9 us
  transfers between devices with their start and end apart: 37, of which 30 were waited for; matrix products, arithmetic and copies ran while one was open for 29% of the time, Pallas kernels for 0%

profile of v1, /device:TPU:0, one launch (start us, length us, event | category | flops | bytes accessed | tf_op | source)
XLA Modules:
  0.0 2096.6 jit_solution(8159988051339093203)
XLA Ops:
  13.3 12.0 collective-permute-done.1
  27.4 22.6 %collective-permute-done.2 = bf16[288,1728]{1,0:T(8,128)(2,1)} collective-permute-done((bf16[288,1728]{1,0:T(8,128)(2,1)S(1)}, bf16[288,1728]{1,0:T(8,128)(2,1)}, u32[]{:S(2)}, u32[]{:S(2)}) %collective-permute-start.2) | collective-permute-done | bytes 995360 | tf_op jit(solution)/shard_map/ppermute | solution.py:15
  54.9 88.3 %collective-permute-done.3 = bf16[576,1728]{1,0:T(8,128)(2,1)} collective-permute-done((bf16[576,1728]{1,0:T(8,128)(2,1)S(1)}, bf16[576,1728]{1,0:T(8,128)(2,1)}, u32[]{:S(2)}, u32[]{:S(2)}) %collective-permute-start.3) | collective-permute-done | bytes 1990688 | tf_op jit(solution)/shard_map/ppermute | solution.py:15
  147.7 6.4 copy.145
  160.4 8.0 all-reduce.21
  169.6 84.8 %all-gather.18.cloned.1.call-done = bf16[1152,3456]{0,1:T(8,128)(2,1)} async-done(((bf16[1152,1728]{0,1:T(8,128)(2,1)}), bf16[1152,3456]{0,1:T(8,128)(2,1)}) %all-gather.18.cloned.1.call-update) | async-done | bytes 7962640 | tf_op jit(solution)/shard_map/all_gather | solution.py:85
  260.9 34.9 %all-gather.20.cloned.1.call-done = bf16[1152,576]{1,0:T(8,128)(2,1)} async-done(((bf16[72,576]{1,0:T(8,128)(2,1)}), bf16[1152,576]{1,0:T(8,128)(2,1)}) %all-gather.20.cloned.1.call-update) | async-done | bytes 1327120 | tf_op jit(solution)/shard_map/all_gather | solution.py:80
  311.8 40.0 %all-gather.24.cloned.1.call-done = bf16[1152,2152]{1,0:T(8,128)(2,1)} async-done(((bf16[72,2152]{1,0:T(8,128)(2,1)}), bf16[1152,2152]{1,0:T(8,128)(2,1)}) %all-gather.24.cloned.1.call-update) | async-done | bytes 4958224 | tf_op jit(solution)/shard_map/all_gather | solution.py:81
  351.8 8.4 copy.151
  360.3 47.0 %all-gather.28.cloned.1.call-done = bf16[1152,2152]{1,0:T(8,128)(2,1)} async-done(((bf16[72,2152]{1,0:T(8,128)(2,1)}), bf16[1152,2152]{1,0:T(8,128)(2,1)}) %all-gather.28.cloned.1.call-update) | async-done | bytes 4958224 | tf_op jit(solution)/shard_map/all_gather | solution.py:82
  407.3 8.4 copy.152
  419.3 32.9 %all-reduce.19 = (bf16[1024]{0:T(1024)(128)(2,1)S(1)}, bf16[1024]{0:T(1024)(128)(2,1)S(1)}, bf16[1024]{0:T(1024)(128)(2,1)S(1)}, bf16[1024]{0:T(1024)(128)(2,1)S(1)}) all-reduce(bf16[1024]{0:T(1024)(128)(2,1)S(1)} %dynamic-update-slice.10, bf16[1024]{0:T(1024)(128)(2,1)S(1)} %dynamic-update-slice.12, ...), channel_id=1, replica_groups=mesh['dev'=2,'sa'=16] {'sa'}, use_global_device_ids=true, to_apply=%add.10 | all-reduce | flops 4096 | bytes 16384
  455.5 7.0 all-gather.38.cloned.1.call-done
  481.1 20.8 all-gather.22.cloned.1.call-done
  506.1 52.1 %all-gather.40.cloned.1.call-done = bf16[1024,2304]{1,0:T(8,128)(2,1)} async-done(((bf16[64,2304]{1,0:T(8,128)(2,1)}), bf16[1024,2304]{1,0:T(8,128)(2,1)}) %all-gather.40.cloned.1.call-update) | async-done | bytes 4718608 | tf_op jit(solution)/shard_map/all_gather | solution.py:128
  580.9 32.1 %all-gather.42.cloned.1.call-done = bf16[1024,2304]{1,0:T(8,128)(2,1)} async-done(((bf16[64,2304]{1,0:T(8,128)(2,1)}), bf16[1024,2304]{1,0:T(8,128)(2,1)}) %all-gather.42.cloned.1.call-update) | async-done | bytes 4718608 | tf_op jit(solution)/shard_map/all_gather | solution.py:128
  641.6 94.9 %all-gather.26.cloned.1.call-done = bf16[1152,4304]{0,1:T(8,128)(2,1)} async-done(((bf16[1152,2152]{0,1:T(8,128)(2,1)}), bf16[1152,4304]{0,1:T(8,128)(2,1)}) %all-gather.26.cloned.1.call-update) | async-done | bytes 9916432 | tf_op jit(solution)/shard_map/all_gather | solution.py:87
  736.5 7.8 convolution_add_fusion.14
  744.3 116.9 %all-gather.30.cloned.1.call-done = bf16[1152,4304]{0,1:T(8,128)(2,1)} async-done(((bf16[1152,2152]{0,1:T(8,128)(2,1)}), bf16[1152,4304]{0,1:T(8,128)(2,1)}) %all-gather.30.cloned.1.call-update) | async-done | bytes 9916432 | tf_op jit(solution)/shard_map/all_gather | solution.py:88
  861.2 7.9 convert_reduce_fusion.6
  916.3 21.3 %copy.193 = bf16[1,1024,2304]{2,0,1:T(2,128)(2,1)} copy(bf16[1,1024,2304]{1,2,0:T(8,128)(2,1)} %pad_maximum_fusion.1) | data formatting | bytes 9437184
  937.7 6.6 copy.287
  957.7 21.5 %copy.195 = bf16[1,1024,2304]{2,0,1:T(2,128)(2,1)} copy(bf16[1,1024,2304]{1,2,0:T(8,128)(2,1)} %pad_maximum_fusion.2) | data formatting | bytes 9437184
  979.2 6.6 copy.286
  999.2 21.8 %copy.197 = bf16[1,1024,2304]{2,0,1:T(2,128)(2,1)} copy(bf16[1,1024,2304]{1,2,0:T(8,128)(2,1)} %pad_maximum_fusion.3) | data formatting | bytes 9437184
  1021.0 6.5 copy.285
  1027.7 6.4 copy.170
  1056.1 43.0 %reduce-scatter.64.cloned.1.call-done = bf16[64,2304]{1,0:T(8,128)(2,1)} async-done(((bf16[1024,2304]{1,0:T(8,128)(2,1)}), bf16[64,2304]{1,0:T(8,128)(2,1)}) %reduce-scatter.64.cloned.1.call-update) | async-done | bytes 294928
  1103.3 74.1 %reduce-scatter.66.cloned.1.call-done = bf16[64,2304]{1,0:T(8,128)(2,1)} async-done(((bf16[1024,2304]{1,0:T(8,128)(2,1)}), bf16[64,2304]{1,0:T(8,128)(2,1)}) %reduce-scatter.66.cloned.1.call-update) | async-done | bytes 294928
  1181.6 95.6 %all-gather.34.cloned.1.call-done = bf16[1152,3456]{0,1:T(8,128)(2,1)} async-done(((bf16[1152,1728]{0,1:T(8,128)(2,1)}), bf16[1152,3456]{0,1:T(8,128)(2,1)}) %all-gather.34.cloned.1.call-update) | async-done | bytes 7962640 | tf_op jit(solution)/shard_map/all_gather | solution.py:175
  1295.3 50.5 %all-gather.36.cloned.1.call-done = bf16[1024,2304]{1,0:T(8,128)(2,1)} async-done(((bf16[64,2304]{1,0:T(8,128)(2,1)}), bf16[1024,2304]{1,0:T(8,128)(2,1)}) %all-gather.36.cloned.1.call-update) | async-done | bytes 4718608 | tf_op jit(solution)/shard_map/all_gather | solution.py:128
  1369.9 7.0 convolution_add_fusion.15
  1376.9 7.9 convert_reduce_fusion.7
  1406.2 21.6 %copy.191 = bf16[1,1024,2304]{2,0,1:T(2,128)(2,1)} copy(bf16[1,1024,2304]{1,2,0:T(8,128)(2,1)} %pad_maximum_fusion) | data formatting | bytes 9437184
  1427.8 6.7 copy.288
  1436.3 8.6 fusion.245
  1445.0 13.0 convolution_add_fusion.5
  1458.1 13.4 convolution_add_fusion.4
  1471.5 13.5 fusion
  1486.7 8.4 fusion.201
  1495.1 12.7 convolution_add_fusion.2
  1510.1 12.9 convolution_add_fusion.1
  1524.9 14.0 fusion.2
  1538.8 14.1 copy.205
  1562.6 11.0 fusion.156
  1573.6 8.7 convolution_add_fusion.8
  1582.4 8.5 convolution_add_fusion.7
  1590.9 11.1 fusion.3
  1614.0 9.0 all-reduce.20
  1623.1 6.9 fusion.29
  1630.0 6.6 fusion.30
  1648.0 6.4 fusion.31
  1654.4 15.1 reduce-scatter.58.cloned.1.call-done
  1684.6 12.8 reduce-scatter.78.cloned.1.call-done
  1699.0 12.8 reduce-scatter.80.cloned.1.call-done
  1713.4 12.6 reduce-scatter.70.cloned.1.call-done
  1727.8 119.4 %reduce-scatter.72.cloned.1.call-done = bf16[72,4304]{1,0:T(8,128)(2,1)} async-done(((bf16[1152,4304]{1,0:T(8,128)(2,1)}), bf16[72,4304]{1,0:T(8,128)(2,1)}) %reduce-scatter.72.cloned.1.call-update) | async-done | bytes 619792
  1855.4 96.2 %reduce-scatter.90.cloned.1.call-done = bf16[72,3456]{1,0:T(8,128)(2,1)} async-done(((bf16[1152,3456]{1,0:T(8,128)(2,1)}), bf16[72,3456]{1,0:T(8,128)(2,1)}) %reduce-scatter.90.cloned.1.call-update) | async-done | bytes 497680
  1955.9 9.6 reduce-scatter.82.cloned.1.call-done
  1966.6 13.3 reduce-scatter.84.cloned.1.call-done
  1980.9 13.9 reduce-scatter.76.cloned.1.call-done
  1995.8 13.7 reduce-scatter.74.cloned.1.call-done
  2010.6 63.4 %all-reduce.18 = (f32[1,576]{1,0:T(1,128)}, f32[1,576]{1,0:T(1,128)}, f32[1,576]{1,0:T(1,128)}, f32[1,576]{1,0:T(1,128)}, f32[1,576]{1,0:T(1,128)}, /*index=5*/f...) all-reduce(bf16[1,576]{1,0:T(2,128)(2,1)S(1)} %copy.208, ...), channel_id=1, replica_groups=mesh['dev'=2,'sa'=16] {'sa'}, use_global_device_ids=true, to_apply=%region_61.62 | all-reduce | flops 6760 | bytes 44864 | tf_op jit(solution)/shard_map/psum | solution.py:353
  2078.1 9.2 reduce-scatter.68.cloned.1.call-done
  (825 shorter events, 374.4 us)
Async XLA Ops:
  7.2 247.1 %all-gather.18.cloned.1.call-start = ((), (), s32[]{:S(2)}) async-start(), calls=%async_computation.19 | async-start | bytes 11943936 | tf_op jit(solution)/shard_map/all_gather | solution.py:85
  7.2 1.9 collective-permute-start
  10.3 15.0 collective-permute-start.1
  25.6 24.5 %collective-permute-start.2 = (bf16[288,1728]{1,0:T(8,128)(2,1)S(1)}, bf16[288,1728]{1,0:T(8,128)(2,1)}, u32[]{:S(2)}, u32[]{:S(2)}) collective-permute-start(bf16[288,1728]{1,0:T(8,128)(2,1)S(1)} %maximum_select_fusion.2), channel_id=1, source_target_pairs={{0,4},{1,5},{2,6},{3,7},{4,0},{5,1},{6,2},{7,3},{8,12},{9,13},{10,... | collective-permute-start | bytes 2985992 | tf_op jit(solution)/shard_map/ppermute | solution.py:15
  52.3 90.9 %collective-permute-start.3 = (bf16[576,1728]{1,0:T(8,128)(2,1)S(1)}, bf16[576,1728]{1,0:T(8,128)(2,1)}, u32[]{:S(2)}, u32[]{:S(2)}) collective-permute-start(bf16[576,1728]{1,0:T(8,128)(2,1)S(1)} %maximum_select_fusion.1), channel_id=1, source_target_pairs={{0,8},{1,9},{2,10},{3,11},{4,12},{5,13},{6,14},{7,15},{8,0},{9,1},... | collective-permute-start | bytes 5971976 | tf_op jit(solution)/shard_map/ppermute | solution.py:15
  154.2 141.6 %all-gather.20.cloned.1.call-start = ((), (), s32[]{:S(2)}) async-start(), calls=%async_computation.20 | async-start | bytes 1566720 | tf_op jit(solution)/shard_map/all_gather | solution.py:80
  155.0 196.8 %all-gather.24.cloned.1.call-start = ((), (), s32[]{:S(2)}) async-start(), calls=%async_computation.22 | async-start | bytes 5326848 | tf_op jit(solution)/shard_map/all_gather | solution.py:81
  155.7 251.6 %all-gather.28.cloned.1.call-start = ((), (), s32[]{:S(2)}) async-start(), calls=%async_computation.24 | async-start | bytes 5326848 | tf_op jit(solution)/shard_map/all_gather | solution.py:82
  156.3 306.2 %all-gather.38.cloned.1.call-start = ((), (), s32[]{:S(2)}) async-start(), calls=%async_computation.30 | async-start | bytes 5013504 | tf_op jit(solution)/shard_map/all_gather | solution.py:128
  168.5 136.7 %copy-start.89 = (f32[1152]{0:T(1024)}, f32[1152]{0:T(1024)S(1)}, u32[]{:S(2)}) copy-start(f32[1152]{0:T(1024)S(1)} %mul.941) | copy-start | bytes 13828
  168.5 136.7 %copy-start.106 = (f32[1152]{0:T(1024)}, f32[1152]{0:T(1024)S(1)}, u32[]{:S(2)}) copy-start(f32[1152]{0:T(1024)S(1)} %add.879) | copy-start | bytes 13828
  168.5 136.7 %copy-start.115 = (f32[3456]{0:T(1024)}, f32[3456]{0:T(1024)S(1)}, u32[]{:S(2)}) copy-start(f32[3456]{0:T(1024)S(1)} %pad_maximum_fusion.18) | copy-start | bytes 41476
  169.2 129.4 %copy-start.161 = (f32[64]{0:T(128)}, f32[64]{0:T(128)S(1)}, u32[]{:S(2)}) copy-start(f32[64]{0:T(128)S(1)} %broadcast_multiply_fusion.3) | copy-start | bytes 772
  169.2 90.9 %copy-start.153 = (f32[64]{0:T(128)}, f32[64]{0:T(128)S(1)}, u32[]{:S(2)}) copy-start(f32[64]{0:T(128)S(1)} %get-tuple-element.231) | copy-start | bytes 772
  169.2 136.0 %copy-start.156 = (f32[64]{0:T(128)}, f32[64]{0:T(128)S(1)}, u32[]{:S(2)}) copy-start(f32[64]{0:T(128)S(1)} %get-tuple-element.230) | copy-start | bytes 772
  169.5 90.6 %copy-start.222 = (f32[64]{0:T(128)}, f32[64]{0:T(128)S(1)}, u32[]{:S(2)}) copy-start(f32[64]{0:T(128)S(1)} %get-tuple-element.108) | copy-start | bytes 772
  169.5 129.0 %copy-start.218 = (f32[64]{0:T(128)}, f32[64]{0:T(128)S(1)}, u32[]{:S(2)}) copy-start(f32[64]{0:T(128)S(1)} %get-tuple-element.110) | copy-start | bytes 772
  169.5 135.6 %copy-start.220 = (f32[64]{0:T(128)}, f32[64]{0:T(128)S(1)}, u32[]{:S(2)}) copy-start(f32[64]{0:T(128)S(1)} %get-tuple-element.109) | copy-start | bytes 772
  169.5 90.5 %copy-start.187 = (f32[64]{0:T(128)}, f32[64]{0:T(128)S(1)}, u32[]{:S(2)}) copy-start(f32[64]{0:T(128)S(1)} %fusion.219) | copy-start | bytes 772
  260.9 241.1 %all-gather.22.cloned.1.call-start = ((), (), s32[]{:S(2)}) async-start(), calls=%async_computation.21 | async-start | bytes 3981312 | tf_op jit(solution)/shard_map/all_gather | solution.py:86
  298.5 259.7 %all-gather.40.cloned.1.call-start = ((), (), s32[]{:S(2)}) async-start(), calls=%async_computation.31 | async-start | bytes 5013504 | tf_op jit(solution)/shard_map/all_gather | solution.py:128
  305.1 308.0 %all-gather.42.cloned.1.call-start = ((), (), s32[]{:S(2)}) async-start(), calls=%async_computation.32 | async-start | bytes 5013504 | tf_op jit(solution)/shard_map/all_gather | solution.py:128
  311.8 424.7 %all-gather.26.cloned.1.call-start = ((), (), s32[]{:S(2)}) async-start(), calls=%async_computation.23 | async-start | bytes 14874624 | tf_op jit(solution)/shard_map/all_gather | solution.py:87
  360.2 501.0 %all-gather.30.cloned.1.call-start = ((), (), s32[]{:S(2)}) async-start(), calls=%async_computation.25 | async-start | bytes 14874624 | tf_op jit(solution)/shard_map/all_gather | solution.py:88
  415.7 611.9 %all-gather.32.cloned.1.call-start = ((), (), s32[]{:S(2)}) async-start(), calls=%async_computation.26 | async-start | bytes 4386816 | tf_op jit(solution)/shard_map/all_gather | solution.py:169
  416.5 635.5 %reduce-scatter.62.cloned.1.call-start = ((), (), s32[]{:S(2)}) async-start(), calls=%async_computation.34 | async-start | bytes 5013504
  417.2 84.8 %copy-start.117 = (f32[1152]{0:T(1024)}, f32[1152]{0:T(1024)S(1)}, u32[]{:S(2)}) copy-start(f32[1152]{0:T(1024)S(1)} %add.880) | copy-start | bytes 13828
  454.4 116.4 %copy-start.83 = (bf16[64,16,72]{2,1,0:T(8,128)(2,1)}, bf16[64,16,72]{2,1,0:T(8,128)(2,1)S(1)}, u32[]{:S(2)}) copy-start(bf16[64,16,72]{2,1,0:T(8,128)(2,1)S(1)} %reshape.1191) | copy-start | bytes 442372
  481.1 81.9 %copy-start.102 = (bf16[64,1152]{1,0:T(8,128)(2,1)}, bf16[64,1152]{1,0:T(8,128)(2,1)S(1)}, u32[]{:S(2)}) copy-start(bf16[64,1152]{1,0:T(8,128)(2,1)S(1)} %convert_element_type.513) | copy-start | bytes 442372
  579.1 320.9 %copy-start.21 = (f32[64,1152]{1,0:T(8,128)}, f32[64,1152]{1,0:T(8,128)S(1)}, u32[]{:S(2)}) copy-start(f32[64,1152]{1,0:T(8,128)S(1)} %get-tuple-element.203) | copy-start | bytes 884740
  944.3 154.9 %reduce-scatter.64.cloned.1.call-start = ((), (), s32[]{:S(2)}) async-start(), calls=%async_computation.35 | async-start | bytes 5013504
  985.8 191.6 %reduce-scatter.66.cloned.1.call-start = ((), (), s32[]{:S(2)}) async-start(), calls=%async_computation.36 | async-start | bytes 5013504
  1027.6 249.6 %all-gather.34.cloned.1.call-start = ((), (), s32[]{:S(2)}) async-start(), calls=%async_computation.27 | async-start | bytes 11943936 | tf_op jit(solution)/shard_map/all_gather | solution.py:175
  1034.1 311.7 %all-gather.36.cloned.1.call-start = ((), (), s32[]{:S(2)}) async-start(), calls=%async_computation.29 | async-start | bytes 5013504 | tf_op jit(solution)/shard_map/all_gather | solution.py:128
  1040.5 244.1 %copy-start.51 = (bf16[1,64,16,72]{1,3,2,0:T(8,128)(2,1)}, bf16[1,64,16,72]{1,3,2,0:T(8,128)(2,1)S(1)}, u32[]{:S(2)}) copy-start(bf16[1,64,16,72]{1,3,2,0:T(8,128)(2,1)S(1)} %copy.188) | copy-start | bytes 442372
  1292.3 230.7 %reduce-scatter.92.cloned.1.call-start = ((), (), s32[]{:S(2)}) async-start(), calls=%async_computation.50 | async-start | bytes 2820096
  1369.6 66.7 %copy-start.30 = (f32[64,1152]{1,0:T(8,128)}, f32[64,1152]{1,0:T(8,128)S(1)}, u32[]{:S(2)}) copy-start(f32[64,1152]{1,0:T(8,128)S(1)} %get-tuple-element.221) | copy-start | bytes 884740
  1394.4 163.9 %reduce-scatter.60.cloned.1.call-start = ((), (), s32[]{:S(2)}) async-start(), calls=%async_computation.33 | async-start | bytes 5013504
  1434.6 169.0 %reduce-scatter.88.cloned.1.call-start = ((), (), s32[]{:S(2)}) async-start(), calls=%async_computation.47 | async-start | bytes 442368
  1436.3 233.2 %reduce-scatter.58.cloned.1.call-start = ((), (), s32[]{:S(2)}) async-start(), calls=%async_computation.28 | async-start | bytes 10653696 | tf_op jit(solution)/shard_map/reduce_scatter | solution.py:304
  1485.0 198.0 %reduce-scatter.86.cloned.1.call-start = ((), (), s32[]{:S(2)}) async-start(), calls=%async_computation.46 | async-start | bytes 442368
  1507.9 189.5 %reduce-scatter.78.cloned.1.call-start = ((), (), s32[]{:S(2)}) async-start(), calls=%async_computation.42 | async-start | bytes 442368
  1509.0 202.9 %reduce-scatter.80.cloned.1.call-start = ((), (), s32[]{:S(2)}) async-start(), calls=%async_computation.43 | async-start | bytes 442368
  1510.0 216.0 %reduce-scatter.70.cloned.1.call-start = ((), (), s32[]{:S(2)}) async-start(), calls=%async_computation.38 | async-start | bytes 442368
  1524.8 322.4 %reduce-scatter.72.cloned.1.call-start = ((), (), s32[]{:S(2)}) async-start(), calls=%async_computation.39 | async-start | bytes 10653696
  1553.0 398.7 %reduce-scatter.90.cloned.1.call-start = ((), (), s32[]{:S(2)}) async-start(), calls=%async_computation.49 | async-start | bytes 8460288
  1602.1 363.5 %reduce-scatter.82.cloned.1.call-start = ((), (), s32[]{:S(2)}) async-start(), calls=%async_computation.44 | async-start | bytes 442368
  1638.9 341.0 %reduce-scatter.84.cloned.1.call-start = ((), (), s32[]{:S(2)}) async-start(), calls=%async_computation.45 | async-start | bytes 442368
  1644.9 349.9 %reduce-scatter.76.cloned.1.call-start = ((), (), s32[]{:S(2)}) async-start(), calls=%async_computation.41 | async-start | bytes 442368
  1646.9 362.6 %reduce-scatter.74.cloned.1.call-start = ((), (), s32[]{:S(2)}) async-start(), calls=%async_computation.40 | async-start | bytes 442368
  1647.9 426.0 %all-reduce.24.cloned.1.call-start = ((), (), s32[]{:S(2)}) async-start(), calls=%async_computation.48 | async-start | bytes 1253376
  1669.6 406.4 %reduce-scatter.94.cloned.1.call-start = ((), (), s32[]{:S(2)}) async-start(), calls=%async_computation.51 | async-start | bytes 1652736
  1675.5 178.2 %copy-start.50 = (bf16[4,64,1152]{2,1,0:T(8,128)(2,1)S(1)}, bf16[4,64,1152]{2,1,0:T(8,128)(2,1)}, u32[]{:S(2)}) copy-start(bf16[4,64,1152]{2,1,0:T(8,128)(2,1)} %param.18) | copy-start | bytes 1769476
  1675.5 178.2 %copy-start.74 = (f32[64,1152]{1,0:T(8,128)S(1)}, f32[64,1152]{1,0:T(8,128)}, u32[]{:S(2)}) copy-start(f32[64,1152]{1,0:T(8,128)} %copy-done.73) | copy-start | bytes 884740
  1675.5 178.2 %copy-start.76 = (f32[64,1152]{1,0:T(8,128)S(1)}, f32[64,1152]{1,0:T(8,128)}, u32[]{:S(2)}) copy-start(f32[64,1152]{1,0:T(8,128)} %copy-done.75) | copy-start | bytes 884740
  1675.5 178.2 %copy-start.78 = (f32[64,1152]{1,0:T(8,128)S(1)}, f32[64,1152]{1,0:T(8,128)}, u32[]{:S(2)}) copy-start(f32[64,1152]{1,0:T(8,128)} %copy-done.77) | copy-start | bytes 884740
  1675.5 178.2 %copy-start.79 = (f32[64,1152]{1,0:T(8,128)S(1)}, f32[64,1152]{1,0:T(8,128)}, u32[]{:S(2)}) copy-start(f32[64,1152]{1,0:T(8,128)} %get-tuple-element.217) | copy-start | bytes 884740
  1849.5 104.4 %copy-start.56 = (f32[64,1152]{1,0:T(8,128)S(1)}, f32[64,1152]{1,0:T(8,128)}, u32[]{:S(2)}) copy-start(f32[64,1152]{1,0:T(8,128)} %copy-done.54) | copy-start | bytes 884740
  1849.5 104.4 %copy-start.62 = (f32[64,1152]{1,0:T(8,128)S(1)}, f32[64,1152]{1,0:T(8,128)}, u32[]{:S(2)}) copy-start(f32[64,1152]{1,0:T(8,128)} %copy-done.61) | copy-start | bytes 884740
  1849.5 104.4 %copy-start.70 = (f32[64,1152]{1,0:T(8,128)S(1)}, f32[64,1152]{1,0:T(8,128)}, u32[]{:S(2)}) copy-start(f32[64,1152]{1,0:T(8,128)} %copy-done.69) | copy-start | bytes 884740
  1849.6 104.4 %copy-start.72 = (f32[64,1152]{1,0:T(8,128)S(1)}, f32[64,1152]{1,0:T(8,128)}, u32[]{:S(2)}) copy-start(f32[64,1152]{1,0:T(8,128)} %copy-done.71) | copy-start | bytes 884740
  1849.6 237.7 %reduce-scatter.68.cloned.1.call-start = ((), (), s32[]{:S(2)}) async-start(), calls=%async_computation.37 | async-start | bytes 1327104
  1855.4 99.6 %copy-start.109 = (bf16[1,64,1152]{2,1,0:T(8,128)(2,1)S(1)}, bf16[1,64,1152]{2,1,0:T(8,128)(2,1)}, u32[]{:S(2)}) copy-start(bf16[1,64,1152]{2,1,0:T(8,128)(2,1)} %get-tuple-element.166) | copy-start | bytes 442372
  1855.4 99.6 %copy-start.110 = (bf16[1,64,1152]{2,1,0:T(8,128)(2,1)S(1)}, bf16[1,64,1152]{2,1,0:T(8,128)(2,1)}, u32[]{:S(2)}) copy-start(bf16[1,64,1152]{2,1,0:T(8,128)(2,1)} %get-tuple-element.167) | copy-start | bytes 442372
  (215 other events, 1590.8 us)
Sparse Core Ops, SparseCore 0:
  154.4 99.9 all-gather.17
  256.5 39.3 all-gather.19
  298.0 53.7 all-gather.23
  353.8 53.4 all-gather.27
  410.0 52.4 all-gather.37
  463.9 37.9 all-gather.21
  504.8 53.3 all-gather.39
  561.1 51.9 all-gather.41
  614.6 121.7 all-gather.25
  737.9 123.2 all-gather.29
  863.5 50.1 all-gather.31
  944.4 75.7 reduce-scatter.61
  1024.5 74.5 reduce-scatter.63
  1102.8 74.5 reduce-scatter.65
  1178.9 98.2 all-gather.33
  1292.4 53.3 all-gather.35
  1394.5 62.4 reduce-scatter.91
  1460.6 74.3 reduce-scatter.59
  1537.4 11.0 reduce-scatter.87
  1553.1 116.3 reduce-scatter.57
  1671.8 11.1 reduce-scatter.85
  1685.4 12.0 reduce-scatter.77
  1699.8 12.0 reduce-scatter.79
  1714.0 12.0 reduce-scatter.69
  1730.8 116.3 reduce-scatter.71
  1851.7 99.8 reduce-scatter.89
  1953.7 11.8 reduce-scatter.81
  1967.8 12.0 reduce-scatter.83
  1982.7 12.0 reduce-scatter.75
  1997.4 12.0 reduce-scatter.73
  2011.8 30.8 all-reduce.23
  2045.0 21.4 reduce-scatter.93
  2068.7 18.5 reduce-scatter.67
